TPU v7x, 32 devices: a whole 2x2x4 slice. The times are simulated.
32 devices in a mesh: fish: 4 (over y, core), curve: 8 (over z, x).
Axes of the slice: x: 2, y: 2, z: 4, core: 2. Of those that a mesh axis runs over, the one named last changes fastest.
Arguments:
- right_side: float32 [128, 128, 128], P('curve', 'fish'), may hold values from -36 to 36
- block_inverse: float32 [512, 512], replicated, may hold values from -1 to 1
- midline: float32 [7, 16, 256], P(None, 'fish'), may hold values from -2 to 10, as said below
- entry_fish: int32 [2048], P(('fish', 'curve')), may hold values from 0 to 3
- entry_seg: int32 [2048], P(('fish', 'curve')), may hold values from 0 to 240
- entry_dest: int32 [2048, 1], P(('fish', 'curve')), may hold values from 0 to 7; in each aligned block of 64 rows (0 to 63, 64 to 127, ...) at most 16 rows name the same one
- entry_block: int32 [2048], P(('fish', 'curve')), may hold values from 0 to 127
Outputs:
- pressure: float32 [128, 128, 128], P('curve', 'fish')
- residual: float32 [128, 128, 128], P('curve', 'fish')
- obstacle: bfloat16 [4, 128, 128, 128], P(None, 'curve', 'fish')
Inputs may be any that keep to these rules, and one draw needn't show every extreme that they name: `midline`: positions lie within a few cells of the block that an entry names; half-widths are positive. `entry_dest`: within the 64 rows of one device no value appears more than 16 times, and in some devices' rows one value appears exactly 16 times.
All inputs are finite; a program needn't handle non-finite values.
Results may differ from a plain program's by a relative error of at most 0.004.
Values may be sent and summed in bfloat16 or wider, within the bound.
A program may use at most 64 MiB of HBM per device.

v0:
```python
import functools
import jax
import jax.numpy as jnp
from jax import lax
from jax.experimental import pallas as pl
from jax.experimental.pallas import tpu as pltpu
from jax.sharding import PartitionSpec as P

BE = 8
SEG = 16
PENALTY = 4.0
F32 = jnp.float32
BF16 = jnp.bfloat16
MESH = pl.DeviceIdType.MESH


def nt_dot(a, b):
    return lax.dot_general(a, b, (((1,), (1,)), ((), ())), preferred_element_type=F32)


def nn_dot(a, b):
    return lax.dot_general(a, b, (((1,), (0,)), ((), ())), preferred_element_type=F32)


def split3(x):
    hi = x.astype(BF16)
    rest = x - hi.astype(F32)
    mid = rest.astype(BF16)
    low = (rest - mid.astype(F32)).astype(BF16)
    return hi, mid, low


def swap_bits(arrays, lane):
    arrays = list(arrays)
    lanes = lane.shape[-1]
    for step in (4, 2, 1):
        clear = (lane & step) == 0
        for a in range(8):
            if a & step:
                continue
            low, high = arrays[a], arrays[a | step]
            arrays[a] = jnp.where(clear, low, pltpu.roll(high, step, axis=1))
            arrays[a | step] = jnp.where(clear, pltpu.roll(low, lanes - step, axis=1), high)
    return arrays


def kernel(
    nf, nc, cap, npts,
    rs_ref, inv_ref, table_ref, meta_ref,
    press_ref, resid_ref, obst_ref,
    mh, ml, gath, shifted, pt, dyz, ob, src, diag,
    y1, v1, m1, w1, n1, u1, m2, w2,
    xsend, zsend, xlow, xhigh, zlow, zhigh, rsend, rfish, rcurve,
    gsend_sem, grecv_sem, hsend_sem, hrecv_sem, fsend_sem, frecv_sem, csend_sem, crecv_sem,
):
    mf = lax.axis_index("fish")
    mc = lax.axis_index("curve")
    cells, lanes = src.shape
    slab = BE * BE
    bx_n = rs_ref.shape[0] // BE
    bz_n = rs_ref.shape[1] // BE
    group = bx_n * bz_n

    barrier = pltpu.get_barrier_semaphore()

    def greet_fish(k, _):
        pl.semaphore_signal(
            barrier, inc=1, device_id=(lax.rem(mf + k, nf), mc), device_id_type=MESH
        )
        return 0

    def greet_curve(k, _):
        pl.semaphore_signal(
            barrier, inc=1, device_id=(mf, lax.rem(mc + k, nc)), device_id_type=MESH
        )
        return 0

    xlow[...] = jnp.zeros_like(xlow)
    xhigh[...] = jnp.zeros_like(xhigh)
    zlow[...] = jnp.zeros_like(zlow)
    zhigh[...] = jnp.zeros_like(zhigh)
    lax.fori_loop(1, nf, greet_fish, 0)
    lax.fori_loop(1, nc, greet_curve, 0)

    def peers(axis, src_at, dst, send_sem, recv_sem):
        count = nf if axis == "fish" else nc
        me = mf if axis == "fish" else mc

        def copy(k, slot, target):
            device = (target, mc) if axis == "fish" else (mf, target)
            return pltpu.make_async_remote_copy(
                src_ref=src_at,
                dst_ref=dst.at[slot],
                send_sem=send_sem.at[k],
                recv_sem=recv_sem.at[k],
                device_id=device,
                device_id_type=MESH,
            )

        def start():
            def body(k, _):
                copy(k, me, lax.rem(me + k, count)).start()
                return 0

            lax.fori_loop(1, count, body, 0)

        def finish():
            def body(k, _):
                origin = lax.rem(me + count - k, count)
                copy(k, origin, origin).wait()
                return 0

            lax.fori_loop(1, count, body, 0)

        return start, finish

    pl.semaphore_wait(barrier, nf - 1 + nc - 1)
    gstart, gfinish = peers("curve", meta_ref, gath, gsend_sem, grecv_sem)
    gath[mc] = meta_ref[...]
    gstart()

    lane8 = lax.broadcasted_iota(jnp.int32, (BE, lanes), 1)
    lane64 = lax.broadcasted_iota(jnp.int32, (slab, lanes), 1)
    lane32 = lax.broadcasted_iota(jnp.int32, (slab // 2, lanes), 1)
    sub8 = lax.broadcasted_iota(jnp.int32, (BE, lanes), 0)

    table = table_ref[...]
    width = table.shape[1]
    for m in range(SEG):
        turned = table if m == 0 else pltpu.roll(table, width - m, axis=1)
        shifted[m * 8 : m * 8 + 8, :] = turned

    whole = inv_ref[...]
    hi = whole.astype(BF16)
    mh[...] = hi
    ml[...] = (whole - hi.astype(F32)).astype(BF16)

    def field_to_rows(read, out_ref):
        parts = []
        for g in range(group):
            bx, bz = g // bz_n, g % bz_n
            parts.append(read(bx, bz).reshape(slab, lanes))
        for j, rows in enumerate(swap_bits(parts, lane64)):
            out_ref[pl.ds(j, slab, stride=BE), :] = rows

    def rows_to_field(read_j, write):
        parts = swap_bits([read_j(j) for j in range(BE)], lane64)
        for bx in range(bx_n):
            for i in range(BE):
                plane = jnp.concatenate(
                    [parts[bx * bz_n + bz][i * BE : (i + 1) * BE, :] for bz in range(bz_n)], axis=0
                )
                write(bx * BE + i, plane)

    field_to_rows(
        lambda bx, bz: rs_ref[bx * BE : (bx + 1) * BE, bz * BE : (bz + 1) * BE, :], src
    )

    gfinish()

    col = lax.broadcasted_iota(jnp.int32, (lanes, lanes), 1)
    row = lax.broadcasted_iota(jnp.int32, (lanes, lanes), 0)
    earlier = jnp.where(row < col, 1.0, 0.0).astype(BF16)
    mine = gath[:, 2, :] == mc.astype(F32)
    rank = nn_dot(jnp.where(mine, 1.0, 0.0).astype(BF16), earlier)
    origin = lax.broadcasted_iota(jnp.int32, (nc, lanes), 0).astype(F32)
    slot = jnp.where(mine, origin * cap + rank, -1.0)
    rowf = row.astype(F32)
    picked = jnp.zeros((8, lanes), F32)
    for c in range(nc):
        hot = jnp.where(rowf == slot[c : c + 1, :], 1.0, 0.0).astype(BF16)
        picked = picked + nt_dot(gath[c].astype(BF16), hot)
    index = picked[0:1, :] * npts + picked[1:2, :]
    place = picked[3:4, :] - 1.0
    block_hot = jnp.where(rowf == place, 1.0, 0.0).astype(BF16)
    point_hot = jnp.where(
        lax.broadcasted_iota(jnp.int32, (width, lanes), 0).astype(F32) == index, 1.0, 0.0
    ).astype(BF16)
    hi, mid, low = split3(shifted[...])
    pt[...] = (nn_dot(hi, point_hot) + nn_dot(mid, point_hot)) + nn_dot(low, point_hot)

    cell = lax.broadcasted_iota(jnp.int32, (slab, lanes), 0)
    zc = (cell // BE).astype(F32) + 0.5
    yc = (cell % BE).astype(F32) + 0.5
    for m in range(SEG):
        dy = yc - pt[m * 8 + 1 : m * 8 + 2, :]
        dz = zc - pt[m * 8 + 2 : m * 8 + 3, :]
        dyz[m] = dy * dy + dz * dz

    half = slab // 2

    def build(i, _):
        xc = i.astype(F32) + 0.5
        for h in range(2):
            lo_row = h * half
            near = ws = vx = vy = vz = None
            for m in range(SEG):
                dx = xc - pt[m * 8 : m * 8 + 1, :]
                d = dyz[m, lo_row : lo_row + half, :] + dx * dx
                e = d + 0.25
                signed = e * lax.rsqrt(e) - pt[m * 8 + 6 : m * 8 + 7, :]
                a = 1.0 / (1.0 + d)
                ax = a * pt[m * 8 + 3 : m * 8 + 4, :]
                ay = a * pt[m * 8 + 4 : m * 8 + 5, :]
                az = a * pt[m * 8 + 5 : m * 8 + 6, :]
                if m == 0:
                    near, ws, vx, vy, vz = signed, a, ax, ay, az
                else:
                    near = jnp.minimum(near, signed)
                    ws, vx, vy, vz = ws + a, vx + ax, vy + ay, vz + az
            ind = 0.5 - 0.5 * jnp.tanh(near)
            scale = 1.0 / ws
            pay = jnp.concatenate(
                [ind, ind * (vx * scale), ind * (vy * scale), ind * (vz * scale)], axis=0
            ).astype(BF16)
            summed = nt_dot(pay, block_hot).astype(BF16).astype(F32)
            base = pl.multiple_of(i * slab + lo_row, half)
            for c in range(4):
                ob[c, pl.ds(base, half), :] = summed[c * half : (c + 1) * half, :]
        return 0

    lax.fori_loop(0, BE, build, 0)
    diag[...] = 6.0 + PENALTY * ob[0]
    src[...] = src[...] - ((ob[1] + ob[2]) + ob[3])

    def precondition(value, out_ref):
        vh = value.astype(BF16)
        vl = (value - vh.astype(F32)).astype(BF16)
        wide = nn_dot(mh[...], jnp.concatenate([vh, vl], axis=1))
        out_ref[...] = (wide[:, :lanes] + wide[:, lanes:]) + nn_dot(ml[...], vh)

    bz8 = lane8 % bz_n
    bx8 = (lane8 // bz_n) % bx_n
    bx64 = (lane64 // bz_n) % bx_n
    bx32 = (lane32 // bz_n) % bx_n

    def turn(x, shift):
        shift = shift % lanes
        return x if shift == 0 else pltpu.roll(x, shift, axis=1)

    def halo(turn_no):
        def copy(buf, dst, k, device):
            return pltpu.make_async_remote_copy(
                src_ref=buf,
                dst_ref=dst.at[turn_no],
                send_sem=hsend_sem.at[turn_no, k],
                recv_sem=hrecv_sem.at[turn_no, k],
                device_id=device,
                device_id_type=MESH,
            )

        down_c = copy(xsend.at[turn_no, 0], xhigh, 0, (mf, lax.max(mc - 1, 0)))
        up_c = copy(xsend.at[turn_no, 1], xlow, 1, (mf, lax.min(mc + 1, nc - 1)))
        down_f = copy(zsend.at[turn_no, 0], zhigh, 2, (lax.max(mf - 1, 0), mc))
        up_f = copy(zsend.at[turn_no, 1], zlow, 3, (lax.min(mf + 1, nf - 1), mc))
        return down_c, up_c, down_f, up_f

    def operate(v_ref, out_ref, turn_no):
        v0 = v_ref[0:slab, :]
        v7 = v_ref[cells - slab : cells, :]
        xsend[turn_no, 0] = jnp.where(bx32 == 0, v0[:half], turn(v0[half:], bz_n))
        xsend[turn_no, 1] = jnp.where(bx32 == 0, turn(v7[:half], -bz_n), v7[half:])
        for t in range(2):
            lowp = highp = None
            for a in range(bz_n):
                start = (t * bz_n + a) * slab
                lo = turn(v_ref[start : start + BE, :], a)
                hg = turn(v_ref[start + slab - BE : start + slab, :], a - (bz_n - 1))
                lowp = lo if a == 0 else jnp.where(bz8 == a, lo, lowp)
                highp = hg if a == 0 else jnp.where(bz8 == a, hg, highp)
            zsend[turn_no, 0, t * BE : (t + 1) * BE, :] = lowp
            zsend[turn_no, 1, t * BE : (t + 1) * BE, :] = highp
        down_c, up_c, down_f, up_f = halo(turn_no)
        has = (mc > 0, mc < nc - 1, mf > 0, mf < nf - 1)
        for cond, cp in zip(has, (down_c, up_c, down_f, up_f)):
            pl.when(cond)(cp.start)

        for i in range(BE):
            v = v_ref[i * slab : (i + 1) * slab, :]
            if i > 0:
                beside = v_ref[(i - 1) * slab : i * slab, :]
            else:
                beside = jnp.where(bx64 > 0, turn(v7, bz_n), 0.0)
            if i < BE - 1:
                beside = beside + v_ref[(i + 1) * slab : (i + 2) * slab, :]
            else:
                beside = beside + jnp.where(bx64 < bx_n - 1, turn(v0, -bz_n), 0.0)
            rows = []
            for k in range(BE):
                t = v[k * BE : (k + 1) * BE, :]
                if k > 0:
                    s = v[(k - 1) * BE : k * BE, :]
                else:
                    s = jnp.where(bz8 > 0, turn(v[slab - BE :, :], 1), 0.0)
                if k < BE - 1:
                    s = s + v[(k + 1) * BE : (k + 2) * BE, :]
                else:
                    s = s + jnp.where(bz8 < bz_n - 1, turn(v[:BE, :], -1), 0.0)
                down = pltpu.roll(t, 1, axis=0)
                edge = jnp.where(lane8 < group, 0.0, turn(down, group))
                s = s + jnp.where(sub8 == 0, edge, down)
                up = pltpu.roll(t, BE - 1, axis=0)
                edge = jnp.where(lane8 >= lanes - group, 0.0, turn(up, -group))
                s = s + jnp.where(sub8 == BE - 1, edge, up)
                rows.append(s)
            beside = beside + jnp.concatenate(rows, axis=0)
            out_ref[i * slab : (i + 1) * slab, :] = (
                diag[i * slab : (i + 1) * slab, :] * v - beside
            )

        for cond, cp in zip((has[1], has[0], has[3], has[2]), (down_c, up_c, down_f, up_f)):
            pl.when(cond)(cp.wait_recv)
        for cond, cp in zip(has, (down_c, up_c, down_f, up_f)):
            pl.when(cond)(cp.wait_send)

        got = xhigh[turn_no]
        for h, part in enumerate((turn(got, bz_n), got)):
            a = cells - slab + h * half
            out_ref[a : a + half, :] = out_ref[a : a + half, :] - jnp.where(
                bx32 == bx_n - 1, part, 0.0
            )
        got = xlow[turn_no]
        for h, part in enumerate((got, turn(got, -bz_n))):
            a = h * half
            out_ref[a : a + half, :] = out_ref[a : a + half, :] - jnp.where(bx32 == 0, part, 0.0)
        for t in range(2):
            gl = zlow[turn_no, t * BE : (t + 1) * BE, :]
            gh = zhigh[turn_no, t * BE : (t + 1) * BE, :]
            for a in range(bz_n):
                start = (t * bz_n + a) * slab
                out_ref[start : start + BE, :] = out_ref[start : start + BE, :] - jnp.where(
                    bz8 == 0, turn(gl, -a), 0.0
                )
                b = start + slab - BE
                out_ref[b : b + BE, :] = out_ref[b : b + BE, :] - jnp.where(
                    bz8 == bz_n - 1, turn(gh, bz_n - 1 - a), 0.0
                )

    def pack(pairs):
        rows = [jnp.sum(a * b, axis=0, keepdims=True) for a, b in pairs]
        rows += [jnp.zeros((1, lanes), F32)] * (8 - len(rows))
        return jnp.concatenate(rows, axis=0)

    def reduction(no):
        fstart, ffinish = peers(
            "fish", rsend.at[no, 0], rfish.at[no], fsend_sem.at[no], frecv_sem.at[no]
        )
        cstart, cfinish = peers(
            "curve", rsend.at[no, 1], rcurve.at[no], csend_sem.at[no], crecv_sem.at[no]
        )

        def first(tile):
            rsend[no, 0] = tile
            rfish[no, mf] = tile
            fstart()

        def second():
            ffinish()
            tile = jnp.sum(rfish[no], axis=0)
            rsend[no, 1] = tile
            rcurve[no, mc] = tile
            cstart()

        def last():
            cfinish()
            tile = jnp.sum(rcurve[no], axis=0)
            total = jnp.sum(tile, axis=1, keepdims=True)
            return [total[r : r + 1, :] for r in range(8)]

        return first, second, last

    precondition(src[...], y1)
    operate(y1, v1, 0)
    precondition(v1[...], m1)
    operate(m1, w1, 1)
    first, second, last = reduction(0)
    r, v, w = src[...], v1[...], w1[...]
    first(pack([(r, r), (r, v), (v, v), (v, w), (w, w), (r, w)]))
    precondition(w1[...], n1)
    second()
    operate(n1, u1, 2)
    for c in range(4):
        def write(x, plane, c=c):
            obst_ref[c, x] = plane.astype(BF16)

        rows_to_field(lambda j, c=c: ob[c, pl.ds(j, slab, stride=BE), :], write)
    rr, rv, vv, vw, ww, rw, _, _ = last()
    alpha = rr / rv
    ts = (rv - alpha * vv) - alpha * (rw - alpha * vw)
    tt = (vv - alpha * vw) - alpha * (vw - alpha * ww)
    omega = ts / tt
    rho2 = (rr - alpha * rv) - omega * (rv - alpha * rw)
    beta = rho2 / rr * (alpha / omega)

    both, prod = alpha + omega, alpha * omega
    r = src[...]
    v, w = v1[...], w1[...]
    r2 = r - both * v + prod * w
    q = v - both * w + prod * u1[...]
    v2 = q + beta * (v - omega * w)
    mr2 = y1[...] - both * m1[...] + prod * n1[...]
    y2 = mr2 + beta * (y1[...] - omega * m1[...])
    n1[...] = alpha * y1[...] + omega * (y1[...] - alpha * m1[...])
    diag_keep = diag
    y1[...] = y2
    m1[...] = mr2
    w1[...] = r2
    u1[...] = q
    v1[...] = v2
    precondition(v2, m2)
    operate(m2, w2, 3)
    r2, q, v2, w = w1[...], u1[...], v1[...], w2[...]
    first, second, last = reduction(1)
    first(
        pack([(src[...], v2), (q, r2), (q, v2), (w, r2), (w, v2), (q, q), (q, w), (w, w)])
    )
    second()
    sv, qr, qv, wr, wv, qq, qw, ww = last()
    alpha2 = rho2 / sv
    ts = (qr - alpha2 * qv) - alpha2 * (wr - alpha2 * wv)
    tt = (qq - alpha2 * qw) - alpha2 * (qw - alpha2 * ww)
    omega2 = ts / tt
    src[...] = n1[...] + alpha2 * y1[...] + omega2 * (m1[...] - alpha2 * m2[...])
    diag_keep[...] = (w1[...] - alpha2 * v1[...]) - omega2 * (u1[...] - alpha2 * w2[...])

    def write_press(x, plane):
        press_ref[x] = plane

    def write_resid(x, plane):
        resid_ref[x] = plane

    rows_to_field(lambda j: src[pl.ds(j, slab, stride=BE), :], write_press)
    rows_to_field(lambda j: diag_keep[pl.ds(j, slab, stride=BE), :], write_resid)


def local(right_side, block_inverse, midline, entry_fish, entry_seg, entry_dest, entry_block):
    nf, nc = lax.axis_size("fish"), lax.axis_size("curve")
    count = entry_fish.shape[0]
    cap = max(2, 2 * count // nc)
    cx, cz, ny = right_side.shape
    lanes = (cx // BE) * (cz // BE) * (ny // BE)
    cells = BE**3
    slab = BE * BE
    rows, fishes, npts = midline.shape
    nyb = ny // BE
    group = (cx // BE) * (cz // BE)
    place = entry_block % nyb * group + entry_block // nyb
    meta = jnp.stack([entry_fish, entry_seg, entry_dest[:, 0], place + 1]).astype(F32)
    meta = jnp.pad(meta, ((0, 4), (0, lanes - count)), constant_values=-1.0)
    table = jnp.pad(midline.reshape(rows, fishes * npts), ((0, 8 - rows), (0, 0)))
    width = fishes * npts
    vmem = pl.BlockSpec(memory_space=pltpu.VMEM)
    big = pltpu.VMEM((cells, lanes), F32)
    dma = pltpu.SemaphoreType.DMA
    return pl.pallas_call(
        functools.partial(kernel, nf, nc, cap, npts),
        out_shape=(
            jax.ShapeDtypeStruct((cx, cz, ny), F32),
            jax.ShapeDtypeStruct((cx, cz, ny), F32),
            jax.ShapeDtypeStruct((4, cx, cz, ny), BF16),
        ),
        in_specs=[vmem] * 4,
        out_specs=(vmem, vmem, vmem),
        scratch_shapes=[
            pltpu.VMEM((cells, cells), BF16),
            pltpu.VMEM((cells, cells), BF16),
            pltpu.VMEM((nc, 8, lanes), F32),
            pltpu.VMEM((SEG * 8, width), F32),
            pltpu.VMEM((SEG * 8, lanes), F32),
            pltpu.VMEM((SEG, slab, lanes), F32),
            pltpu.VMEM((4, cells, lanes), F32),
        ]
        + [big] * 10
        + [
            pltpu.VMEM((4, 2, slab // 2, lanes), F32),
            pltpu.VMEM((4, 2, 2 * BE, lanes), F32),
            pltpu.VMEM((4, slab // 2, lanes), F32),
            pltpu.VMEM((4, slab // 2, lanes), F32),
            pltpu.VMEM((4, 2 * BE, lanes), F32),
            pltpu.VMEM((4, 2 * BE, lanes), F32),
            pltpu.VMEM((2, 2, 8, lanes), F32),
            pltpu.VMEM((2, nf, 8, lanes), F32),
            pltpu.VMEM((2, nc, 8, lanes), F32),
            dma((nc,)),
            dma((nc,)),
            dma((4, 4)),
            dma((4, 4)),
            dma((2, nf)),
            dma((2, nf)),
            dma((2, nc)),
            dma((2, nc)),
        ],
        compiler_params=pltpu.CompilerParams(collective_id=0, has_side_effects=True),
    )(right_side, block_inverse, table, meta)


def solution(mesh):
    return jax.shard_map(
        local,
        mesh=mesh,
        in_specs=(
            P("curve", "fish", None),
            P(),
            P(None, "fish", None),
            P(("fish", "curve")),
            P(("fish", "curve")),
            P(("fish", "curve"), None),
            P(("fish", "curve")),
        ),
        out_specs=(
            P("curve", "fish", None),
            P("curve", "fish", None),
            P(None, "curve", "fish", None),
        ),
        check_vma=False,
    )
```

profile of v0, /device:TPU:0, one launch (start us, length us, event | category | flops | bytes accessed | tf_op | source)
XLA Modules:
  0.0 50.5 jit_solution(14401611247762927256)
XLA Ops:
  0.6 0.0 copy-start.5
  0.6 0.6 %copy-done.5 = s32[64]{0:T(128)S(1)} copy-done((s32[64]{0:T(128)S(1)}, s32[64]{0:T(128)}, u32[]{:S(2)}) %copy-start.5) | copy-done | bytes 280
  1.3 0.0 copy-start.2
  1.3 0.0 copy-start.3
  1.3 0.0 copy-start.4
  1.3 0.6 %copy-done.2 = s32[64,1]{0,1:T(1,128)S(1)} copy-done((s32[64,1]{0,1:T(1,128)S(1)}, s32[64,1]{0,1:T(1,128)}, u32[]{:S(2)}) %copy-start.2) | copy-done | bytes 280
  1.9 0.0 copy-done.3
  2.0 0.0 copy-done.4
  2.0 0.6 %pad.9.meta_ref = f32[8,128]{1,0:T(8,128)} pad(f32[4,64]{1,0:T(4,128)S(1)} %add_convert_fusion, f32[]{:T(128)} %constant.35.clone.1), padding=0_4x0_64 | pad | bytes 5124 | tf_op jit(solution)/shard_map/jit(_pad)/pad | solution.py:449
  2.6 0.8 %copy.10 = f32[1,7,4,256]{3,1,2,0:T(8,128)S(1)} copy(f32[1,7,4,256]{3,2,1,0:T(4,128)} %bitcast.8) | data formatting | bytes 57344
  3.3 0.6 %pad.8.table_ref = f32[8,1024]{1,0:T(8,128)} pad(f32[7,1024]{1,0:T(8,128)S(1)} %bitcast.7, f32[]{:T(128)} %constant.27.clone.1), padding=0_1x0_0 | pad | bytes 61444 | tf_op jit(solution)/shard_map/jit(_pad)/pad | solution.py:450
  4.0 43.3 %shard_map.94 = (f32[16,32,128]{2,1,0:T(8,128)}, f32[16,32,128]{2,1,0:T(8,128)}, bf16[4,16,32,128]{3,2,1,0:T(8,128)(2,1)}) custom-call(f32[16,32,128]{2,1,0:T(8,128)} %rs_ref.1, f32[512,512]{1,0:T(8,128)} %inv_ref.1, f32[8,1024]{1,0:T(8,128)} %pad.8.table_ref, f32[8,128]{1,0:T(8,128)} %pad.9.meta_ref), custom_call_target="tpu_custom_call" | custom-call | tf_op jit(solution)/shard_map/pallas_call | solution.py:455
  47.2 0.0 copy-start.1
  47.2 0.0 copy-start
  47.3 1.7 %copy.14 = f32[16,32,128]{2,1,0:T(8,128)} copy(f32[16,32,128]{2,1,0:T(8,128)} %get-tuple-element.6) | data formatting | bytes 524288
  49.0 0.0 copy-done.1
  49.0 0.7 %copy.15 = f32[16,32,128]{2,1,0:T(8,128)} copy(f32[16,32,128]{2,1,0:T(8,128)S(1)} %copy-done.1) | data formatting | bytes 524288
  49.7 0.0 copy-done
  49.7 0.8 %copy.16 = bf16[4,16,32,128]{3,2,1,0:T(8,128)(2,1)} copy(bf16[4,16,32,128]{3,2,1,0:T(8,128)(2,1)S(1)} %copy-done) | data formatting | bytes 1048576
  (2 shorter events, 0.0 us)
Async XLA Ops:
  0.6 0.7 %copy-start.5 = (s32[64]{0:T(128)S(1)}, s32[64]{0:T(128)}, u32[]{:S(2)}) copy-start(s32[64]{0:T(128)} %param.13) | copy-start | bytes 772
  1.3 0.7 %copy-start.2 = (s32[64,1]{0,1:T(1,128)S(1)}, s32[64,1]{0,1:T(1,128)}, u32[]{:S(2)}) copy-start(s32[64,1]{0,1:T(1,128)} %param.12) | copy-start | bytes 772
  1.3 0.7 %copy-start.3 = (s32[64]{0:T(128)S(1)}, s32[64]{0:T(128)}, u32[]{:S(2)}) copy-start(s32[64]{0:T(128)} %param.11) | copy-start | bytes 772
  1.3 0.7 %copy-start.4 = (s32[64]{0:T(128)S(1)}, s32[64]{0:T(128)}, u32[]{:S(2)}) copy-start(s32[64]{0:T(128)} %param.10) | copy-start | bytes 772
  47.2 1.8 %copy-start.1 = (f32[16,32,128]{2,1,0:T(8,128)S(1)}, f32[16,32,128]{2,1,0:T(8,128)}, u32[]{:S(2)}) copy-start(f32[16,32,128]{2,1,0:T(8,128)} %get-tuple-element.7) | copy-start | bytes 786436
  47.2 2.5 %copy-start = (bf16[4,16,32,128]{3,2,1,0:T(8,128)(2,1)S(1)}, bf16[4,16,32,128]{3,2,1,0:T(8,128)(2,1)}, u32[]{:S(2)}) copy-start(bf16[4,16,32,128]{3,2,1,0:T(8,128)(2,1)} %get-tuple-element.8) | copy-start | bytes 1572868
where the time goes:
time: 50.7 us; the launch traced here: 50.5 us
  Pallas kernels  43.3 us (85%)
  local copies, waits for them, and re-layouts  6.54 us (13%)
  between operations  0.67 us (1%)
    pallas_call x1, Pallas kernels, local(): pl.pallas_call(functools.partial(kernel, nf, nc, cap, npts), out_shape=(j...  43.3 us
    unnamed x16, local copies, waits for them, and re-layouts  5.32 us

commit v1 on v0

--- a/solution.py
+++ b/solution.py
@@ -46,9 +46,9 @@
 
 def kernel(
     nf, nc, cap, npts,
-    rs_ref, inv_ref, table_ref, meta_ref,
+    rs_ref, inv_ref, mid_ref, fish_ref, seg_ref, dest_ref, block_ref,
     press_ref, resid_ref, obst_ref,
-    mh, ml, gath, shifted, pt, dyz, ob, src, diag,
+    mh, ml, rhs, meta_ref, tab, gath, shifted, pt, dyz, ob, src, diag,
     y1, v1, m1, w1, n1, u1, m2, w2,
     xsend, zsend, xlow, xhigh, zlow, zhigh, rsend, rfish, rcurve,
     gsend_sem, grecv_sem, hsend_sem, hrecv_sem, fsend_sem, frecv_sem, csend_sem, crecv_sem,
@@ -75,6 +75,13 @@
         )
         return 0
 
+    nyb = rs_ref.shape[2] // BE
+    count = fish_ref.shape[1]
+    meta_ref[...] = jnp.full_like(meta_ref, -1.0)
+    block = block_ref[...]
+    place_in = block % nyb * group + block // nyb + 1
+    for r, column in enumerate((fish_ref[...], seg_ref[...], dest_ref[...], place_in)):
+        meta_ref[r : r + 1, 0:count] = column.astype(F32)
     xlow[...] = jnp.zeros_like(xlow)
     xhigh[...] = jnp.zeros_like(xhigh)
     zlow[...] = jnp.zeros_like(zlow)
@@ -124,16 +131,23 @@
     lane32 = lax.broadcasted_iota(jnp.int32, (slab // 2, lanes), 1)
     sub8 = lax.broadcasted_iota(jnp.int32, (BE, lanes), 0)
 
-    table = table_ref[...]
-    width = table.shape[1]
+    rows, fishes, _ = mid_ref.shape
+    width = tab.shape[1]
+    for f in range(fishes):
+        tab[0:rows, f * npts : (f + 1) * npts] = mid_ref[:, f, :]
+    tab[rows:8, :] = jnp.zeros((8 - rows, width), F32)
+    table = tab[...]
     for m in range(SEG):
         turned = table if m == 0 else pltpu.roll(table, width - m, axis=1)
         shifted[m * 8 : m * 8 + 8, :] = turned
 
     whole = inv_ref[...]
     hi = whole.astype(BF16)
-    mh[...] = hi
-    ml[...] = (whole - hi.astype(F32)).astype(BF16)
+    low = (whole - hi.astype(F32)).astype(BF16)
+    for full, kept in ((hi, mh), (low, ml)):
+        kept[0:slab, :] = full[0:slab, :]
+        kept[slab : 2 * slab, :] = full[cells - slab :, :]
+        kept[2 * slab :, :] = full[slab : cells - slab, :]
 
     def field_to_rows(read, out_ref):
         parts = []
@@ -223,11 +237,9 @@
     diag[...] = 6.0 + PENALTY * ob[0]
     src[...] = src[...] - ((ob[1] + ob[2]) + ob[3])
 
-    def precondition(value, out_ref):
-        vh = value.astype(BF16)
-        vl = (value - vh.astype(F32)).astype(BF16)
-        wide = nn_dot(mh[...], jnp.concatenate([vh, vl], axis=1))
-        out_ref[...] = (wide[:, :lanes] + wide[:, lanes:]) + nn_dot(ml[...], vh)
+    def product(a, b):
+        wide = nn_dot(mh[a:b, :], rhs[...])
+        return (wide[:, :lanes] + wide[:, lanes:]) + nn_dot(ml[a:b, :], rhs[:, :lanes])
 
     bz8 = lane8 % bz_n
     bx8 = (lane8 // bz_n) % bx_n
@@ -255,11 +267,21 @@
         up_f = copy(zsend.at[turn_no, 1], zlow, 3, (lax.min(mf + 1, nf - 1), mc))
         return down_c, up_c, down_f, up_f
 
-    def operate(v_ref, out_ref, turn_no):
-        v0 = v_ref[0:slab, :]
-        v7 = v_ref[cells - slab : cells, :]
+    def apply(value, v_ref, out_ref, turn_no, between=None):
+        down_c, up_c, down_f, up_f = halo(turn_no)
+        has = (mc > 0, mc < nc - 1, mf > 0, mf < nf - 1)
+        vh = value.astype(BF16)
+        rhs[:, :lanes] = vh
+        rhs[:, lanes:] = (value - vh.astype(F32)).astype(BF16)
+        ends = product(0, 2 * slab)
+        v0, v7 = ends[:slab], ends[slab:]
+        v_ref[0:slab, :] = v0
+        v_ref[cells - slab : cells, :] = v7
         xsend[turn_no, 0] = jnp.where(bx32 == 0, v0[:half], turn(v0[half:], bz_n))
         xsend[turn_no, 1] = jnp.where(bx32 == 0, turn(v7[:half], -bz_n), v7[half:])
+        for cond, cp in zip(has[:2], (down_c, up_c)):
+            pl.when(cond)(cp.start)
+        v_ref[slab : cells - slab, :] = product(2 * slab, cells)
         for t in range(2):
             lowp = highp = None
             for a in range(bz_n):
@@ -270,11 +292,13 @@
                 highp = hg if a == 0 else jnp.where(bz8 == a, hg, highp)
             zsend[turn_no, 0, t * BE : (t + 1) * BE, :] = lowp
             zsend[turn_no, 1, t * BE : (t + 1) * BE, :] = highp
-        down_c, up_c, down_f, up_f = halo(turn_no)
-        has = (mc > 0, mc < nc - 1, mf > 0, mf < nf - 1)
-        for cond, cp in zip(has, (down_c, up_c, down_f, up_f)):
+        for cond, cp in zip(has[2:], (down_f, up_f)):
             pl.when(cond)(cp.start)
-
+        if between is not None:
+            between()
+
+        v0 = v_ref[0:slab, :]
+        v7 = v_ref[cells - slab : cells, :]
         for i in range(BE):
             v = v_ref[i * slab : (i + 1) * slab, :]
             if i > 0:
@@ -369,16 +393,12 @@
 
         return first, second, last
 
-    precondition(src[...], y1)
-    operate(y1, v1, 0)
-    precondition(v1[...], m1)
-    operate(m1, w1, 1)
+    apply(src[...], y1, v1, 0)
+    apply(v1[...], m1, w1, 1)
     first, second, last = reduction(0)
     r, v, w = src[...], v1[...], w1[...]
     first(pack([(r, r), (r, v), (v, v), (v, w), (w, w), (r, w)]))
-    precondition(w1[...], n1)
-    second()
-    operate(n1, u1, 2)
+    apply(w1[...], n1, u1, 2, second)
     for c in range(4):
         def write(x, plane, c=c):
             obst_ref[c, x] = plane.astype(BF16)
@@ -407,8 +427,7 @@
     w1[...] = r2
     u1[...] = q
     v1[...] = v2
-    precondition(v2, m2)
-    operate(m2, w2, 3)
+    apply(v2, m2, w2, 3)
     r2, q, v2, w = w1[...], u1[...], v1[...], w2[...]
     first, second, last = reduction(1)
     first(
@@ -442,12 +461,6 @@
     cells = BE**3
     slab = BE * BE
     rows, fishes, npts = midline.shape
-    nyb = ny // BE
-    group = (cx // BE) * (cz // BE)
-    place = entry_block % nyb * group + entry_block // nyb
-    meta = jnp.stack([entry_fish, entry_seg, entry_dest[:, 0], place + 1]).astype(F32)
-    meta = jnp.pad(meta, ((0, 4), (0, lanes - count)), constant_values=-1.0)
-    table = jnp.pad(midline.reshape(rows, fishes * npts), ((0, 8 - rows), (0, 0)))
     width = fishes * npts
     vmem = pl.BlockSpec(memory_space=pltpu.VMEM)
     big = pltpu.VMEM((cells, lanes), F32)
@@ -459,11 +472,14 @@
             jax.ShapeDtypeStruct((cx, cz, ny), F32),
             jax.ShapeDtypeStruct((4, cx, cz, ny), BF16),
         ),
-        in_specs=[vmem] * 4,
+        in_specs=[vmem] * 7,
         out_specs=(vmem, vmem, vmem),
         scratch_shapes=[
             pltpu.VMEM((cells, cells), BF16),
             pltpu.VMEM((cells, cells), BF16),
+            pltpu.VMEM((cells, 2 * lanes), BF16),
+            pltpu.VMEM((8, lanes), F32),
+            pltpu.VMEM((8, width), F32),
             pltpu.VMEM((nc, 8, lanes), F32),
             pltpu.VMEM((SEG * 8, width), F32),
             pltpu.VMEM((SEG * 8, lanes), F32),
@@ -491,7 +507,12 @@
             dma((2, nc)),
         ],
         compiler_params=pltpu.CompilerParams(collective_id=0, has_side_effects=True),
-    )(right_side, block_inverse, table, meta)
+    )(
+        right_side,
+        block_inverse,
+        midline,
+        *(e.reshape(1, count) for e in (entry_fish, entry_seg, entry_dest, entry_block)),
+    )
 
 
 def solution(mesh):

time: 50.7 us -> 45.7 us (0.901)
  local copies, waits for them, and re-layouts: 6.54 us -> 3.25 us
  Pallas kernels: 43.3 us -> 41.7 us
    unnamed x16 -> x7, local copies, waits for them, and re-layouts: 5.32 us -> 3.25 us
    pallas_call x1, Pallas kernels: 43.3 us -> 41.7 us  [local(): pl.pallas_call(functools.partial(kernel, nf, nc, cap, npts), out_shape=(j...]
    pad x2 -> x0, local copies, waits for them, and re-layouts: 1.22 us -> none  [the longest x1 0.62 us: local(): jnp.pad(midline.reshape(rows, fishes * npts), ((0, 8 - rows), (0, 0)))]
where the time goes in v1:
time: 45.7 us; the launch traced here: 45.6 us
  Pallas kernels  41.7 us (91%)
  local copies, waits for them, and re-layouts  3.25 us (7%)
  between operations  0.66 us (1%)
    pallas_call x1, Pallas kernels, local(): pl.pallas_call(functools.partial(kernel, nf, nc, cap, npts), out_shape=(j...  41.7 us
    unnamed x7, local copies, waits for them, and re-layouts  3.25 us

profile of v1, /device:TPU:0, one launch (start us, length us, event | category | flops | bytes accessed | tf_op | source)
XLA Modules:
  0.0 45.6 jit_solution(4774880850643222136)
XLA Ops:
  0.6 41.7 %shard_map.94 = (f32[16,32,128]{2,1,0:T(8,128)}, f32[16,32,128]{2,1,0:T(8,128)}, bf16[4,16,32,128]{3,2,1,0:T(8,128)(2,1)}) custom-call(f32[16,32,128]{2,1,0:T(8,128)} %rs_ref.1, f32[512,512]{1,0:T(8,128)} %inv_ref.1, f32[7,4,256]{2,1,0:T(4,128)} %mid_ref.1, s32[1,64]{1,0:T(1,128)} %bitcast.4, s32[1,64]{1,0:T(1,128)} %bitcast.5, s32[1,64]{1,0:T(1,128)} %bitcast.6, ...), custom_call_target="tpu_custom_call" | custom-call | tf_op jit(solution)/shard_map/pallas_call | solution.py:468
  42.3 0.0 copy-start.1
  42.3 0.0 copy-start
  42.3 1.7 %copy.13 = f32[16,32,128]{2,1,0:T(8,128)} copy(f32[16,32,128]{2,1,0:T(8,128)} %get-tuple-element.6) | data formatting | bytes 524288
  44.1 0.0 copy-done.1
  44.1 0.7 %copy.14 = f32[16,32,128]{2,1,0:T(8,128)} copy(f32[16,32,128]{2,1,0:T(8,128)S(1)} %copy-done.1) | data formatting | bytes 524288
  44.8 0.0 copy-done
  44.8 0.8 %copy.15 = bf16[4,16,32,128]{3,2,1,0:T(8,128)(2,1)} copy(bf16[4,16,32,128]{3,2,1,0:T(8,128)(2,1)S(1)} %copy-done) | data formatting | bytes 1048576
Async XLA Ops:
  42.3 1.8 %copy-start.1 = (f32[16,32,128]{2,1,0:T(8,128)S(1)}, f32[16,32,128]{2,1,0:T(8,128)}, u32[]{:S(2)}) copy-start(f32[16,32,128]{2,1,0:T(8,128)} %get-tuple-element.7) | copy-start | bytes 786436
  42.3 2.5 %copy-start = (bf16[4,16,32,128]{3,2,1,0:T(8,128)(2,1)S(1)}, bf16[4,16,32,128]{3,2,1,0:T(8,128)(2,1)}, u32[]{:S(2)}) copy-start(bf16[4,16,32,128]{3,2,1,0:T(8,128)(2,1)} %get-tuple-element.8) | copy-start | bytes 1572868

commit v2 on v1

--- a/solution.py
+++ b/solution.py
@@ -44,11 +44,54 @@
     return arrays
 
 
+def rows_to_field(read_j, write, bx_n, bz_n, lane):
+    parts = swap_bits([read_j(j) for j in range(BE)], lane)
+    for bx in range(bx_n):
+        for i in range(BE):
+            plane = jnp.concatenate(
+                [parts[bx * bz_n + bz][i * BE : (i + 1) * BE, :] for bz in range(bz_n)], axis=0
+            )
+            write(bx * BE + i, plane)
+
+
+def finish(
+    prow_ref, rrow_ref, oin_ref, press_ref, resid_ref, obst_ref, prow, rrow, pf, rf, of, sems
+):
+    slab = BE * BE
+    bx_n, bz_n = pf.shape[0] // BE, pf.shape[1] // BE
+    lane = lax.broadcasted_iota(jnp.int32, (slab, prow.shape[1]), 1)
+    take = [
+        pltpu.make_async_copy(a, b, sems.at[n])
+        for n, (a, b) in enumerate(((prow_ref, prow), (rrow_ref, rrow), (oin_ref, of)))
+    ]
+    give = [
+        pltpu.make_async_copy(a, b, sems.at[3 + n])
+        for n, (a, b) in enumerate(((pf, press_ref), (rf, resid_ref), (of, obst_ref)))
+    ]
+    for copy in take:
+        copy.start()
+    for n, (rows, field) in enumerate(((prow, pf), (rrow, rf))):
+        take[n].wait()
+
+        def write(x, plane, field=field):
+            field[x] = plane
+
+        rows_to_field(
+            lambda j, rows=rows: rows[pl.ds(j, slab, stride=BE), :], write, bx_n, bz_n, lane
+        )
+        give[n].start()
+        if n == 0:
+            take[2].wait()
+            give[2].start()
+    for copy in give:
+        copy.wait()
+
+
 def kernel(
     nf, nc, cap, npts,
     rs_ref, inv_ref, mid_ref, fish_ref, seg_ref, dest_ref, block_ref,
     press_ref, resid_ref, obst_ref,
-    mh, ml, rhs, meta_ref, tab, gath, shifted, pt, dyz, ob, src, diag,
+    obf, obf_sem, mh, ml, rhs, meta_ref, tab, gath, shifted, pt, dyz, ob, src, diag,
     y1, v1, m1, w1, n1, u1, m2, w2,
     xsend, zsend, xlow, xhigh, zlow, zhigh, rsend, rfish, rcurve,
     gsend_sem, grecv_sem, hsend_sem, hrecv_sem, fsend_sem, frecv_sem, csend_sem, crecv_sem,
@@ -156,15 +199,6 @@
             parts.append(read(bx, bz).reshape(slab, lanes))
         for j, rows in enumerate(swap_bits(parts, lane64)):
             out_ref[pl.ds(j, slab, stride=BE), :] = rows
-
-    def rows_to_field(read_j, write):
-        parts = swap_bits([read_j(j) for j in range(BE)], lane64)
-        for bx in range(bx_n):
-            for i in range(BE):
-                plane = jnp.concatenate(
-                    [parts[bx * bz_n + bz][i * BE : (i + 1) * BE, :] for bz in range(bz_n)], axis=0
-                )
-                write(bx * BE + i, plane)
 
     field_to_rows(
         lambda bx, bz: rs_ref[bx * BE : (bx + 1) * BE, bz * BE : (bz + 1) * BE, :], src
@@ -401,9 +435,13 @@
     apply(w1[...], n1, u1, 2, second)
     for c in range(4):
         def write(x, plane, c=c):
-            obst_ref[c, x] = plane.astype(BF16)
-
-        rows_to_field(lambda j, c=c: ob[c, pl.ds(j, slab, stride=BE), :], write)
+            obf[c, x] = plane.astype(BF16)
+
+        rows_to_field(
+            lambda j, c=c: ob[c, pl.ds(j, slab, stride=BE), :], write, bx_n, bz_n, lane64
+        )
+    out_copy = pltpu.make_async_copy(obf, obst_ref, obf_sem)
+    out_copy.start()
     rr, rv, vv, vw, ww, rw, _, _ = last()
     alpha = rr / rv
     ts = (rv - alpha * vv) - alpha * (rw - alpha * vw)
@@ -421,7 +459,6 @@
     mr2 = y1[...] - both * m1[...] + prod * n1[...]
     y2 = mr2 + beta * (y1[...] - omega * m1[...])
     n1[...] = alpha * y1[...] + omega * (y1[...] - alpha * m1[...])
-    diag_keep = diag
     y1[...] = y2
     m1[...] = mr2
     w1[...] = r2
@@ -439,17 +476,9 @@
     ts = (qr - alpha2 * qv) - alpha2 * (wr - alpha2 * wv)
     tt = (qq - alpha2 * qw) - alpha2 * (qw - alpha2 * ww)
     omega2 = ts / tt
-    src[...] = n1[...] + alpha2 * y1[...] + omega2 * (m1[...] - alpha2 * m2[...])
-    diag_keep[...] = (w1[...] - alpha2 * v1[...]) - omega2 * (u1[...] - alpha2 * w2[...])
-
-    def write_press(x, plane):
-        press_ref[x] = plane
-
-    def write_resid(x, plane):
-        resid_ref[x] = plane
-
-    rows_to_field(lambda j: src[pl.ds(j, slab, stride=BE), :], write_press)
-    rows_to_field(lambda j: diag_keep[pl.ds(j, slab, stride=BE), :], write_resid)
+    press_ref[...] = n1[...] + alpha2 * y1[...] + omega2 * (m1[...] - alpha2 * m2[...])
+    resid_ref[...] = (w1[...] - alpha2 * v1[...]) - omega2 * (u1[...] - alpha2 * w2[...])
+    out_copy.wait()
 
 
 def local(right_side, block_inverse, midline, entry_fish, entry_seg, entry_dest, entry_block):
@@ -465,16 +494,18 @@
     vmem = pl.BlockSpec(memory_space=pltpu.VMEM)
     big = pltpu.VMEM((cells, lanes), F32)
     dma = pltpu.SemaphoreType.DMA
-    return pl.pallas_call(
+    anywhere = pl.BlockSpec(memory_space=pl.ANY)
+    field = jax.ShapeDtypeStruct((cx, cz, ny), F32)
+    fields = jax.ShapeDtypeStruct((4, cx, cz, ny), BF16)
+    row_form = jax.ShapeDtypeStruct((cells, lanes), F32)
+    solved = pl.pallas_call(
         functools.partial(kernel, nf, nc, cap, npts),
-        out_shape=(
-            jax.ShapeDtypeStruct((cx, cz, ny), F32),
-            jax.ShapeDtypeStruct((cx, cz, ny), F32),
-            jax.ShapeDtypeStruct((4, cx, cz, ny), BF16),
-        ),
+        out_shape=(row_form, row_form, fields),
         in_specs=[vmem] * 7,
-        out_specs=(vmem, vmem, vmem),
+        out_specs=(vmem, vmem, anywhere),
         scratch_shapes=[
+            pltpu.VMEM((4, cx, cz, ny), BF16),
+            dma,
             pltpu.VMEM((cells, cells), BF16),
             pltpu.VMEM((cells, cells), BF16),
             pltpu.VMEM((cells, 2 * lanes), BF16),
@@ -513,6 +544,20 @@
         midline,
         *(e.reshape(1, count) for e in (entry_fish, entry_seg, entry_dest, entry_block)),
     )
+    return pl.pallas_call(
+        finish,
+        out_shape=(field, field, fields),
+        in_specs=[anywhere] * 3,
+        out_specs=(anywhere,) * 3,
+        scratch_shapes=[
+            big,
+            big,
+            pltpu.VMEM((cx, cz, ny), F32),
+            pltpu.VMEM((cx, cz, ny), F32),
+            pltpu.VMEM((4, cx, cz, ny), BF16),
+            dma((6,)),
+        ],
+    )(*solved)
 
 
 def solution(mesh):

time: 45.7 us -> 44.4 us (0.972)
  local copies, waits for them, and re-layouts: 3.25 us -> 0 us
  Pallas kernels: 41.7 us -> 43.6 us
    unnamed x7 -> x0, local copies, waits for them, and re-layouts: 3.25 us -> none
    pallas_call x1 -> x2, Pallas kernels: 41.7 us -> 43.6 us  [the longest x1 41.2 us: local(): pl.pallas_call(functools.partial(kernel, nf, nc, cap, npts), out_shape=(r...]
where the time goes in v2:
time: 44.4 us; the launch traced here: 44.2 us
  Pallas kernels  43.6 us (98%)
  between operations  0.64 us (1%)
    pallas_call x1, Pallas kernels, local(): pl.pallas_call(functools.partial(kernel, nf, nc, cap, npts), out_shape=(r...  41.2 us
    pallas_call x1, Pallas kernels, local(): pl.pallas_call(finish, out_shape=(field, field, fields), in_specs=[anywhe...  2.36 us

profile of v2, /device:TPU:0, one launch (start us, length us, event | category | flops | bytes accessed | tf_op | source)
XLA Modules:
  0.0 44.2 jit_solution(9816549053591940302)
XLA Ops:
  0.6 41.2 %shard_map.94 = (f32[512,128]{1,0:T(8,128)}, f32[512,128]{1,0:T(8,128)}, bf16[4,16,32,128]{3,2,1,0:T(8,128)(2,1)}) custom-call(f32[16,32,128]{2,1,0:T(8,128)} %rs_ref.1, f32[512,512]{1,0:T(8,128)} %inv_ref.1, f32[7,4,256]{2,1,0:T(4,128)} %mid_ref.1, s32[1,64]{1,0:T(1,128)} %bitcast.4, s32[1,64]{1,0:T(1,128)} %bitcast.5, s32[1,64]{1,0:T(1,128)} %bitcast.6, ...), custom_call_target="tpu_custom_call" | custom-call | tf_op jit(solution)/shard_map/pallas_call | solution.py:501
  41.8 2.4 %shard_map.95 = (f32[16,32,128]{2,1,0:T(8,128)}, f32[16,32,128]{2,1,0:T(8,128)}, bf16[4,16,32,128]{3,2,1,0:T(8,128)(2,1)}) custom-call(f32[512,128]{1,0:T(8,128)} %get-tuple-element.6.prow_ref, f32[512,128]{1,0:T(8,128)} %get-tuple-element.7.rrow_ref, bf16[4,16,32,128]{3,2,1,0:T(8,128)(2,1)} %get-tuple-element.8.oin_ref), custom_call_target="tpu_custom_call" | custom-call | tf_op jit(solution)/shard_map/pallas_call | solution.py:547

commit v3 on v2

--- a/solution.py
+++ b/solution.py
@@ -89,9 +89,9 @@
 
 def kernel(
     nf, nc, cap, npts,
-    rs_ref, inv_ref, mid_ref, fish_ref, seg_ref, dest_ref, block_ref,
-    press_ref, resid_ref, obst_ref,
-    obf, obf_sem, mh, ml, rhs, meta_ref, tab, gath, shifted, pt, dyz, ob, src, diag,
+    rs_hbm, inv_hbm, mid_ref, fish_ref, seg_ref, dest_ref, block_ref,
+    press_hbm, resid_hbm, obst_ref,
+    rs_ref, inv_ref, in_sem, obf, obf_sem, mh, ml, rhs, meta_ref, tab, gath, shifted, pt, dyz, ob, src, diag,
     y1, v1, m1, w1, n1, u1, m2, w2,
     xsend, zsend, xlow, xhigh, zlow, zhigh, rsend, rfish, rcurve,
     gsend_sem, grecv_sem, hsend_sem, hrecv_sem, fsend_sem, frecv_sem, csend_sem, crecv_sem,
@@ -103,6 +103,11 @@
     bx_n = rs_ref.shape[0] // BE
     bz_n = rs_ref.shape[1] // BE
     group = bx_n * bz_n
+
+    inv_copy = pltpu.make_async_copy(inv_hbm, inv_ref, in_sem.at[0])
+    rs_copy = pltpu.make_async_copy(rs_hbm, rs_ref, in_sem.at[1])
+    inv_copy.start()
+    rs_copy.start()
 
     barrier = pltpu.get_barrier_semaphore()
 
@@ -184,6 +189,7 @@
         turned = table if m == 0 else pltpu.roll(table, width - m, axis=1)
         shifted[m * 8 : m * 8 + 8, :] = turned
 
+    inv_copy.wait()
     whole = inv_ref[...]
     hi = whole.astype(BF16)
     low = (whole - hi.astype(F32)).astype(BF16)
@@ -200,6 +206,7 @@
         for j, rows in enumerate(swap_bits(parts, lane64)):
             out_ref[pl.ds(j, slab, stride=BE), :] = rows
 
+    rs_copy.wait()
     field_to_rows(
         lambda bx, bz: rs_ref[bx * BE : (bx + 1) * BE, bz * BE : (bz + 1) * BE, :], src
     )
@@ -476,9 +483,15 @@
     ts = (qr - alpha2 * qv) - alpha2 * (wr - alpha2 * wv)
     tt = (qq - alpha2 * qw) - alpha2 * (qw - alpha2 * ww)
     omega2 = ts / tt
-    press_ref[...] = n1[...] + alpha2 * y1[...] + omega2 * (m1[...] - alpha2 * m2[...])
-    resid_ref[...] = (w1[...] - alpha2 * v1[...]) - omega2 * (u1[...] - alpha2 * w2[...])
+    diag[...] = n1[...] + alpha2 * y1[...] + omega2 * (m1[...] - alpha2 * m2[...])
+    press_copy = pltpu.make_async_copy(diag, press_hbm, in_sem.at[0])
+    press_copy.start()
+    src[...] = (w1[...] - alpha2 * v1[...]) - omega2 * (u1[...] - alpha2 * w2[...])
+    resid_copy = pltpu.make_async_copy(src, resid_hbm, in_sem.at[1])
+    resid_copy.start()
     out_copy.wait()
+    press_copy.wait()
+    resid_copy.wait()
 
 
 def local(right_side, block_inverse, midline, entry_fish, entry_seg, entry_dest, entry_block):
@@ -501,9 +514,12 @@
     solved = pl.pallas_call(
         functools.partial(kernel, nf, nc, cap, npts),
         out_shape=(row_form, row_form, fields),
-        in_specs=[vmem] * 7,
-        out_specs=(vmem, vmem, anywhere),
+        in_specs=[anywhere] * 2 + [vmem] * 5,
+        out_specs=(anywhere,) * 3,
         scratch_shapes=[
+            pltpu.VMEM((cx, cz, ny), F32),
+            pltpu.VMEM((cells, cells), F32),
+            dma((2,)),
             pltpu.VMEM((4, cx, cz, ny), BF16),
             dma,
             pltpu.VMEM((cells, cells), BF16),

time: 44.4 us -> 43.8 us (0.986)
  Pallas kernels: 43.6 us -> 43 us
    pallas_call x1, Pallas kernels: 41.2 us -> 40.6 us  [local(): pl.pallas_call(functools.partial(kernel, nf, nc, cap, npts), out_shape=(r...]
where the time goes in v3:
time: 43.8 us; the launch traced here: 43.6 us
  Pallas kernels  43 us (98%)
  between operations  0.64 us (1%)
    pallas_call x1, Pallas kernels, local(): pl.pallas_call(functools.partial(kernel, nf, nc, cap, npts), out_shape=(r...  40.6 us
    pallas_call x1, Pallas kernels, local(): pl.pallas_call(finish, out_shape=(field, field, fields), in_specs=[anywhe...  2.36 us

profile of v3, /device:TPU:0, one launch (start us, length us, event | category | flops | bytes accessed | tf_op | source)
XLA Modules:
  0.0 43.6 jit_solution(17068429411500386616)
XLA Ops:
  0.6 40.6 %shard_map.94 = (f32[512,128]{1,0:T(8,128)}, f32[512,128]{1,0:T(8,128)}, bf16[4,16,32,128]{3,2,1,0:T(8,128)(2,1)}) custom-call(f32[16,32,128]{2,1,0:T(8,128)} %rs_hbm.1, f32[512,512]{1,0:T(8,128)} %inv_hbm.1, f32[7,4,256]{2,1,0:T(4,128)} %mid_ref.1, s32[1,64]{1,0:T(1,128)} %bitcast.4, s32[1,64]{1,0:T(1,128)} %bitcast.5, s32[1,64]{1,0:T(1,128)} %bitcast.6, ...), custom_call_target="tpu_custom_call" | custom-call | tf_op jit(solution)/shard_map/pallas_call | solution.py:514
  41.2 2.4 %shard_map.95 = (f32[16,32,128]{2,1,0:T(8,128)}, f32[16,32,128]{2,1,0:T(8,128)}, bf16[4,16,32,128]{3,2,1,0:T(8,128)(2,1)}) custom-call(f32[512,128]{1,0:T(8,128)} %get-tuple-element.6.prow_ref, f32[512,128]{1,0:T(8,128)} %get-tuple-element.7.rrow_ref, bf16[4,16,32,128]{3,2,1,0:T(8,128)(2,1)} %get-tuple-element.8.oin_ref), custom_call_target="tpu_custom_call" | custom-call | tf_op jit(solution)/shard_map/pallas_call | solution.py:563

commit v4 on v3

--- a/solution.py
+++ b/solution.py
@@ -375,8 +375,6 @@
 
         for cond, cp in zip((has[1], has[0], has[3], has[2]), (down_c, up_c, down_f, up_f)):
             pl.when(cond)(cp.wait_recv)
-        for cond, cp in zip(has, (down_c, up_c, down_f, up_f)):
-            pl.when(cond)(cp.wait_send)
 
         got = xhigh[turn_no]
         for h, part in enumerate((turn(got, bz_n), got)):
@@ -400,6 +398,8 @@
                 out_ref[b : b + BE, :] = out_ref[b : b + BE, :] - jnp.where(
                     bz8 == bz_n - 1, turn(gh, bz_n - 1 - a), 0.0
                 )
+        for cond, cp in zip(has, (down_c, up_c, down_f, up_f)):
+            pl.when(cond)(cp.wait_send)
 
     def pack(pairs):
         rows = [jnp.sum(a * b, axis=0, keepdims=True) for a, b in pairs]

time: 43.8 us -> 44 us (level)
  no operation moved by 1% of the time
where the time goes in v4:
time: 44 us; the launch traced here: 43.8 us
  Pallas kernels  43.2 us (98%)
  between operations  0.64 us (1%)
    pallas_call x1, Pallas kernels, local(): pl.pallas_call(functools.partial(kernel, nf, nc, cap, npts), out_shape=(r...  40.8 us
    pallas_call x1, Pallas kernels, local(): pl.pallas_call(finish, out_shape=(field, field, fields), in_specs=[anywhe...  2.36 us

profile of v4, /device:TPU:0, one launch (start us, length us, event | category | flops | bytes accessed | tf_op | source)
XLA Modules:
  0.0 43.8 jit_solution(6966314777267565926)
XLA Ops:
  0.6 40.8 %shard_map.94 = (f32[512,128]{1,0:T(8,128)}, f32[512,128]{1,0:T(8,128)}, bf16[4,16,32,128]{3,2,1,0:T(8,128)(2,1)}) custom-call(f32[16,32,128]{2,1,0:T(8,128)} %rs_hbm.1, f32[512,512]{1,0:T(8,128)} %inv_hbm.1, f32[7,4,256]{2,1,0:T(4,128)} %mid_ref.1, s32[1,64]{1,0:T(1,128)} %bitcast.4, s32[1,64]{1,0:T(1,128)} %bitcast.5, s32[1,64]{1,0:T(1,128)} %bitcast.6, ...), custom_call_target="tpu_custom_call" | custom-call | tf_op jit(solution)/shard_map/pallas_call | solution.py:514
  41.4 2.4 %shard_map.95 = (f32[16,32,128]{2,1,0:T(8,128)}, f32[16,32,128]{2,1,0:T(8,128)}, bf16[4,16,32,128]{3,2,1,0:T(8,128)(2,1)}) custom-call(f32[512,128]{1,0:T(8,128)} %get-tuple-element.6.prow_ref, f32[512,128]{1,0:T(8,128)} %get-tuple-element.7.rrow_ref, bf16[4,16,32,128]{3,2,1,0:T(8,128)(2,1)} %get-tuple-element.8.oin_ref), custom_call_target="tpu_custom_call" | custom-call | tf_op jit(solution)/shard_map/pallas_call | solution.py:563
